TPU v7x, 32 devices: a whole 2x2x4 slice. The times are simulated.
32 devices in a mesh: group: 2 (over y), expert: 4 (over z), tensor: 4 (over x, core).
Axes of the slice: x: 2, y: 2, z: 4, core: 2. Of those that a mesh axis runs over, the one named last changes fastest.
Arguments:
- tokens: bfloat16 [512, 4096], P(('group', 'expert'), 'tensor'), parts along dimension 0, may hold values from -400 to 400
- norm_gain: float32 [4096], replicated, may hold values from 0.1 to 1.9
- expert_ids: int32 [512, 8], P(('group', 'expert')), parts along dimension 0, may hold values from 0 to 63, all different within a row; in each aligned block of 64 rows (0 to 63, 64 to 127, ...) at most 16 rows name the same one
- gate_weights: float32 [512, 8], P(('group', 'expert')), parts along dimension 0, may hold values from 0.1 to 1
- gate_proj: bfloat16 [64, 768, 4096], P('expert', 'tensor'), may hold values from -0.09375 to 0.09375
- up_proj: bfloat16 [64, 768, 4096], P('expert', 'tensor'), may hold values from -0.09375 to 0.09375
- down_proj: bfloat16 [64, 4096, 768], P('expert', 'tensor'), may hold values from -0.21875 to 0.21875
Outputs:
- moe_out: bfloat16 [512, 4096], P(('group', 'expert'), 'tensor'), parts along dimension 0
There are 2 independent parts, one for each index of `group`. A program takes and returns all parts, laid end to end along the dimension named above; an argument that names none is the same for every part. Nothing has to cross between parts.
Inputs may be any that keep to these rules, and one draw needn't show every extreme that they name: `expert_ids`: each row names 8 different experts. Within the rows of one device (aligned blocks of 64 rows) no expert is named by more than 16 rows, a bound that some block reaches.
All inputs are finite; a program needn't handle non-finite values.
Results may differ from a plain program's by a relative error of at most 0.008.
Values may be sent and summed in bfloat16 or wider, within the bound.
No kernel may reach another device: no remote copies, remote signals or barrier semaphores. Data moves between devices by JAX's collectives and lax.ppermute only.
A program may use at most 128 MiB of HBM per device.

v0:
```python
import jax
import jax.numpy as jnp
from jax import lax
from jax.sharding import PartitionSpec as P

D = 4096
EXPERTS = 64
TOP = 8
CAP = 16
epsilon = 1e-06


def slot_places(expert_ids):
    flat_ids = expert_ids.reshape(-1)
    onehot = (flat_ids[:, None] == jnp.arange(EXPERTS, dtype=jnp.int32)[None, :]).astype(jnp.int32)
    before = jnp.cumsum(onehot, axis=0) - onehot
    inside = jnp.sum(onehot * before, axis=1)
    return flat_ids * CAP + inside


def expert_block(slot_rows, gate_proj, up_proj, down_proj):
    sources = slot_rows.shape[0]
    local_experts = slot_rows.shape[1]
    item_count = slot_rows.shape[2]
    gate_act = jnp.einsum(
        "slcd,lfd->lfsc", slot_rows, gate_proj, preferred_element_type=jnp.float32
    )
    up_act = jnp.einsum("slcd,lfd->lfsc", slot_rows, up_proj, preferred_element_type=jnp.float32)
    hidden = (jax.nn.silu(gate_act) * up_act).astype(jnp.bfloat16)
    hidden = hidden.reshape(local_experts, hidden.shape[1], sources * item_count)
    hidden_all = lax.all_gather(hidden, "tensor", axis=1, tiled=True)
    hidden_all = hidden_all.reshape(local_experts, hidden_all.shape[1], sources, item_count)
    result = jnp.einsum(
        "lfsc,ldf->slcd", hidden_all, down_proj, preferred_element_type=jnp.float32
    ).astype(jnp.bfloat16)
    return lax.all_to_all(result, "expert", split_axis=0, concat_axis=0, tiled=True)


def body(tokens, norm_gain, expert_ids, gate_weights, gate_proj, up_proj, down_proj):
    local_experts = gate_proj.shape[0]
    groups = lax.axis_size("expert")
    tok_rows = tokens.shape[0]
    places = slot_places(expert_ids)
    owners = (
        jnp.full((EXPERTS * CAP,), tok_rows, jnp.int32)
        .at[places]
        .set(jnp.arange(places.shape[0], dtype=jnp.int32) // TOP)
    )
    values = tokens.astype(jnp.float32)
    squares = lax.psum(jnp.sum(values * values, axis=1), "tensor")
    inv_scale = lax.rsqrt(squares / D + epsilon)[:, None]
    quarter_width = tokens.shape[1]
    gain_part = lax.dynamic_slice_in_dim(
        norm_gain, lax.axis_index("tensor") * quarter_width, quarter_width
    )
    normed = (values * inv_scale * gain_part).astype(jnp.bfloat16)
    padded = jnp.concatenate([normed, jnp.zeros((1, quarter_width), jnp.bfloat16)], axis=0)
    dispatched = padded[owners].reshape(groups, local_experts, CAP, quarter_width)
    full_rows = lax.all_gather(
        lax.all_to_all(dispatched, "expert", split_axis=0, concat_axis=0, tiled=True),
        "tensor",
        axis=3,
        tiled=True,
    )
    returned = expert_block(full_rows, gate_proj, up_proj, down_proj)
    out_width = returned.shape[-1]
    flat_back = returned.reshape(EXPERTS * CAP, out_width)
    picked = flat_back[places].reshape(tok_rows, TOP, out_width).astype(jnp.float32)
    return jnp.einsum("tkd,tk->td", picked, gate_weights).astype(jnp.bfloat16)


def solution(mesh):
    return jax.shard_map(
        body,
        mesh=mesh,
        in_specs=(
            P(("group", "expert"), "tensor"),
            P(),
            P(("group", "expert"), None),
            P(("group", "expert"), None),
            P("expert", "tensor", None),
            P("expert", "tensor", None),
            P("expert", "tensor", None),
        ),
        out_specs=P(("group", "expert"), "tensor"),
        check_vma=False,
    )
```

profile of v0, /device:TPU:0, one launch (start us, length us, event | category | flops | bytes accessed | tf_op | source)
XLA Modules:
  0.0 281.1 jit_solution(12578102919068015323)
XLA Ops:
  6.5 0.8 copy.15
  7.3 0.1 eq.29
  7.4 0.1 eq.25
  7.5 0.7 broadcast_multiply_fusion
  8.2 1.2 reduce-window.6
  9.4 0.2 slice_reduce_fusion
  9.7 0.1 copy.14
  9.8 0.1 mul.56
  9.9 0.1 fusion.27
  10.0 2.4 scatter_custom_fusion
  12.5 1.0 fusion.22
  13.5 8.4 %psum.7 = f32[64]{0:T(128)S(1)} all-reduce(f32[64]{0:T(128)S(1)} %fusion.22), channel_id=1, replica_groups=mesh['group'=2,'expert'=4,'tensor'=4] {'tensor'}, use_global_device_ids=true, to_apply=%region_1.2 | all-reduce | flops 64 | bytes 512 | tf_op jit(solution)/shard_map/psum | solution.py:50
  21.9 0.7 dynamic_slice.3
  22.6 1.0 fusion.24
  23.6 4.1 %gather_fusion = bf16[1024,1024]{1,0:T(8,128)(2,1)S(1)} fusion(bf16[65,1024]{1,0:T(8,128)(2,1)S(1)} %concatenate.3, s32[1024]{0:T(1024)S(1)} %fusion.29), kind=kCustom, calls=%fused_computation | custom fusion | bytes 4198400 | tf_op jit(solution)/shard_map/gather | solution.py:58
  27.7 51.7 %all_to_all.10 = bf16[4,16,16,1024]{3,2,1,0:T(8,128)(2,1)S(1)} all-to-all(bf16[4,16,16,1024]{3,2,1,0:T(8,128)(2,1)S(1)} %bitcast.72), channel_id=1, replica_groups=mesh['group'=2,'expert'=4,'tensor'=4] {'expert'}, dimensions={0} | all-to-all | bytes 4194304 | tf_op jit(solution)/shard_map/all_to_all | solution.py:60
  79.3 1.6 copy.18
  80.9 0.2 all-gather.5.cloned.1.call-start
  81.2 57.3 %all-gather.3.cloned.1.call-done = bf16[4,16,16,4096]{3,2,0,1:T(8,128)(2,1)} async-done(((bf16[4,16,16,1024]{3,2,0,1:T(8,128)(2,1)}), bf16[4,16,16,4096]{3,2,0,1:T(8,128)(2,1)}) %all-gather.3.cloned.1.call-update) | async-done | bytes 8388624 | tf_op jit(solution)/shard_map/all_gather | solution.py:59
  138.5 14.8 %fusion.8 = f32[16,192,4,16]{1,3,2,0:T(8,128)S(1)} fusion(bf16[4,16,16,4096]{3,2,0,1:T(8,128)(2,1)} %all-gather.3.cloned.1.call-done, bf16[16,192,4096]{2,1,0:T(8,128)(2,1)} %param.11), kind=kOutput, calls=%fused_computation.10 | convolution fusion | flops 1610612736 | bytes 34340864 | tf_op jit(solution)/shard_map/slcd,lfd->lfsc/dot_general | solution.py:25
  153.3 15.0 %fusion.17 = bf16[16,192,4,16]{1,3,2,0:T(8,128)(2,1)S(1)} fusion(bf16[4,16,16,4096]{3,2,0,1:T(8,128)(2,1)} %all-gather.3.cloned.1.call-done, bf16[16,192,4096]{2,1,0:T(8,128)(2,1)} %param.12, f32[16,192,4,16]{1,3,2,0:T(8,128)S(1)} %fusion.8), kind=kOutput, calls=%fused_computation.13 | convolution fusion | flops 1611792384 | bytes 34734080 | tf_op jit(solution)/shard_map/slcd,lfd->lfsc/dot_general | solution.py:28
  168.3 1.5 copy.19
  169.8 28.7 %all-gather.5.cloned.1.call-done = bf16[16,768,64]{2,0,1:T(8,128)(2,1)} async-done(((bf16[16,192,64]{2,0,1:T(8,128)(2,1)}), bf16[16,768,64]{2,0,1:T(8,128)(2,1)}) %all-gather.5.cloned.1.call-update) | async-done | bytes 1572880 | tf_op jit(solution)/shard_map/all_gather | solution.py:31
  198.5 5.0 %copy.20 = bf16[16,768,64]{1,2,0:T(8,128)(2,1)} copy(bf16[16,768,64]{2,0,1:T(8,128)(2,1)} %all-gather.5.cloned.1.call-done) | data formatting | bytes 3145728 | tf_op jit(solution)/shard_map/all_gather | solution.py:31
  203.5 12.8 %convert_bitcast_fusion = bf16[4,16,16,1024]{3,2,0,1:T(8,128)(2,1)S(1)} fusion(bf16[16,768,4,16]{1,3,2,0:T(8,128)(2,1)} %bitcast.73, bf16[16,1024,768]{2,1,0:T(8,128)(2,1)} %param.13), kind=kOutput, calls=%fused_computation.9 | convolution fusion | flops 1611661312 | bytes 28835840 | tf_op jit(solution)/shard_map/lfsc,ldf->slcd/dot_general | solution.py:33
  216.3 1.5 copy.21
  217.9 4.6 %all-to-all-start.1 = ((bf16[4,16,16,1024]{3,2,1,0:T(8,128)(2,1)}), bf16[4,16,16,1024]{3,2,1,0:T(8,128)(2,1)S(1)}, u32[]{:S(2)}, u32[]{:S(2)}) async-start(bf16[4,16,16,1024]{3,2,1,0:T(8,128)(2,1)} %copy.21), calls=%async_computation.1 | async-start | bytes 4194304 | tf_op jit(solution)/shard_map/all_to_all | solution.py:36
  222.5 0.1 copy.25
  222.6 48.5 %all-to-all-done.1 = bf16[4,16,16,1024]{3,2,1,0:T(8,128)(2,1)S(1)} async-done(((bf16[4,16,16,1024]{3,2,1,0:T(8,128)(2,1)}), bf16[4,16,16,1024]{3,2,1,0:T(8,128)(2,1)S(1)}, u32[]{:S(2)}, u32[]{:S(2)}) %all-to-all-start.1) | async-done | bytes 2097184 | tf_op jit(solution)/shard_map/all_to_all | solution.py:36
  271.1 2.0 gather_fusion.1
  273.1 0.4 fusion.20
  273.5 0.7 copy.30
  (14 shorter events, 0.1 us)
Async XLA Ops:
  6.5 132.0 %all-gather.3.cloned.1.call-start = ((), (), s32[]{:S(2)}) async-start(), calls=%async_computation.2 | async-start | bytes 10485760 | tf_op jit(solution)/shard_map/all_gather | solution.py:59
  80.9 117.5 %all-gather.5.cloned.1.call-start = ((), (), s32[]{:S(2)}) async-start(), calls=%async_computation.3 | async-start | bytes 3932160 | tf_op jit(solution)/shard_map/all_gather | solution.py:31
  216.3 6.2 %copy-start = (f32[64,8]{0,1:T(8,128)S(1)}, f32[64,8]{0,1:T(8,128)}, u32[]{:S(2)}) copy-start(f32[64,8]{0,1:T(8,128)} %param.10) | copy-start | bytes 6148
  217.9 53.2 %all-to-all-start.1 = ((bf16[4,16,16,1024]{3,2,1,0:T(8,128)(2,1)}), bf16[4,16,16,1024]{3,2,1,0:T(8,128)(2,1)S(1)}, u32[]{:S(2)}, u32[]{:S(2)}) async-start(bf16[4,16,16,1024]{3,2,1,0:T(8,128)(2,1)} %copy.21), calls=%async_computation.1 | async-start | bytes 4194304 | tf_op jit(solution)/shard_map/all_to_all | solution.py:36
Sparse Core Ops, SparseCore 0:
  81.1 57.3 all-gather.2
  169.9 28.4 all-gather.4
where the time goes:
time: 282 us; the launch traced here: 281 us
  waiting for transfers between devices  134 us (48%)
  blocking collectives  60 us (21%)
  matrix products  43.1 us (15%)
  local copies, waits for them, and re-layouts  21 us (7%)
  between operations  13.5 us (5%)
  starting transfers between devices  4.82 us (2%)
  other arithmetic  4.13 us (1%)
    all_gather x1, waiting for transfers between devices, body(): lax.all_gather(lax.all_to_all(dispatched, 'expert', split_axis=0, concat_...  57.3 us
    all_to_all x1, blocking collectives, body(): lax.all_to_all(dispatched, 'expert', split_axis=0, concat_axis=0, tiled=T...  51.7 us
    all_to_all x1, waiting for transfers between devices, expert_block(): lax.all_to_all(result, 'expert', split_axis=0, concat_axis=0, tiled=True)  48.5 us
    all_gather x1, waiting for transfers between devices, expert_block(): hidden_all = lax.all_gather(hidden, 'tensor', axis=1, tiled=True)  28.7 us
    dot_general x1, matrix products, expert_block(): jnp.einsum('slcd,lfd->lfsc', slot_rows, up_proj, preferred_element_type=j...  15 us
    dot_general x1, matrix products, expert_block(): jnp.einsum('slcd,lfd->lfsc', slot_rows, gate_proj, preferred_element_type...  14.8 us
    dot_general x1, matrix products, expert_block(): jnp.einsum('lfsc,ldf->slcd', hidden_all, down_proj, preferred_element_typ...  12.8 us
    psum x1, blocking collectives, body(): squares = lax.psum(jnp.sum(values * values, axis=1), 'tensor')  8.37 us
  transfers between devices with their start and end apart: 3, of which 3 were waited for; matrix products, arithmetic and copies ran while one was open for 0% of the time, Pallas kernels for 0%

commit v1 on v0

--- a/solution.py
+++ b/solution.py
@@ -8,6 +8,9 @@
 TOP = 8
 CAP = 16
 epsilon = 1e-06
+resolve_pairs_all_here = lambda row_data: jnp.concatenate(
+    lax.all_gather(row_data, axis_name="tensor"), axis=1
+)
 
 
 def slot_places(expert_ids):
@@ -28,7 +31,7 @@
     up_act = jnp.einsum("slcd,lfd->lfsc", slot_rows, up_proj, preferred_element_type=jnp.float32)
     hidden = (jax.nn.silu(gate_act) * up_act).astype(jnp.bfloat16)
     hidden = hidden.reshape(local_experts, hidden.shape[1], sources * item_count)
-    hidden_all = lax.all_gather(hidden, "tensor", axis=1, tiled=True)
+    hidden_all = resolve_pairs_all_here(hidden)
     hidden_all = hidden_all.reshape(local_experts, hidden_all.shape[1], sources, item_count)
     result = jnp.einsum(
         "lfsc,ldf->slcd", hidden_all, down_proj, preferred_element_type=jnp.float32

time: 282 us -> 276 us (0.979)
  waiting for transfers between devices: 134 us -> 129 us
    all_gather x1, waiting for transfers between devices: 28.7 us -> 22.7 us  [lax.all_gather(row_data, axis_name='tensor')]
    all_gather x1 -> x0, local copies, waits for them, and re-layouts: 4.99 us -> none  [expert_block(): hidden_all = lax.all_gather(hidden, 'tensor', axis=1, tiled=True)]
    another operation x1 -> x2, local copies, waits for them, and re-layouts: 0.01 us -> 2.86 us  [the longest x1 2.86 us: expert_block(): hidden_all.reshape(local_experts, hidden_all.shape[1], sources, item_count)]
where the time goes in v1:
time: 276 us
  waiting for transfers between devices  129 us (47%)
  blocking collectives  60 us (22%)
  matrix products  43.9 us (16%)
  local copies, waits for them, and re-layouts  20.8 us (8%)
  between operations  13.5 us (5%)
  starting transfers between devices  4.82 us (2%)
  other arithmetic  4.13 us (1%)
    all_gather x1, waiting for transfers between devices, body(): lax.all_gather(lax.all_to_all(dispatched, 'expert', split_axis=0, concat_...  57.3 us
    all_to_all x1, blocking collectives, body(): lax.all_to_all(dispatched, 'expert', split_axis=0, concat_axis=0, tiled=T...  51.7 us
    all_to_all x1, waiting for transfers between devices, expert_block(): lax.all_to_all(result, 'expert', split_axis=0, concat_axis=0, tiled=True)  48.5 us
    all_gather x1, waiting for transfers between devices, lax.all_gather(row_data, axis_name='tensor')  22.7 us
    dot_general x1, matrix products, expert_block(): jnp.einsum('slcd,lfd->lfsc', slot_rows, up_proj, preferred_element_type=j...  15.9 us
    dot_general x1, matrix products, expert_block(): jnp.einsum('slcd,lfd->lfsc', slot_rows, gate_proj, preferred_element_type...  14.8 us
    dot_general x1, matrix products, expert_block(): jnp.einsum('lfsc,ldf->slcd', hidden_all, down_proj, preferred_element_typ...  12.8 us
    psum x1, blocking collectives, body(): squares = lax.psum(jnp.sum(values * values, axis=1), 'tensor')  8.37 us
  transfers between devices with their start and end apart: 3, of which 3 were waited for; matrix products, arithmetic and copies ran while one was open for 0% of the time, Pallas kernels for 0%

profile of v1, /device:TPU:0, one launch (start us, length us, event | category | flops | bytes accessed | tf_op | source)
XLA Modules:
  0.0 275.7 jit_solution(10062662104745222131)
XLA Ops:
  6.5 0.8 copy.17
  7.3 0.1 eq.29
  7.4 0.1 eq.25
  7.5 0.7 broadcast_multiply_fusion
  8.2 1.2 reduce-window.6
  9.4 0.2 slice_reduce_fusion
  9.7 0.1 copy.16
  9.8 0.1 mul.56
  9.9 0.1 fusion.27
  10.0 2.4 scatter_custom_fusion
  12.5 1.0 fusion.22
  13.5 8.4 %psum.7 = f32[64]{0:T(128)S(1)} all-reduce(f32[64]{0:T(128)S(1)} %fusion.22), channel_id=1, replica_groups=mesh['group'=2,'expert'=4,'tensor'=4] {'tensor'}, use_global_device_ids=true, to_apply=%region_1.2 | all-reduce | flops 64 | bytes 512 | tf_op jit(solution)/shard_map/psum | solution.py:53
  21.9 0.7 dynamic_slice.3
  22.6 1.0 fusion.24
  23.6 4.1 %gather_fusion = bf16[1024,1024]{1,0:T(8,128)(2,1)S(1)} fusion(bf16[65,1024]{1,0:T(8,128)(2,1)S(1)} %concatenate.3, s32[1024]{0:T(1024)S(1)} %fusion.29), kind=kCustom, calls=%fused_computation | custom fusion | bytes 4198400 | tf_op jit(solution)/shard_map/gather | solution.py:61
  27.7 51.7 %all_to_all.10 = bf16[4,16,16,1024]{3,2,1,0:T(8,128)(2,1)S(1)} all-to-all(bf16[4,16,16,1024]{3,2,1,0:T(8,128)(2,1)S(1)} %bitcast.74), channel_id=1, replica_groups=mesh['group'=2,'expert'=4,'tensor'=4] {'expert'}, dimensions={0} | all-to-all | bytes 4194304 | tf_op jit(solution)/shard_map/all_to_all | solution.py:63
  79.3 1.6 copy.20
  80.9 0.2 all-gather.5.cloned.1.call-start
  81.2 57.3 %all-gather.3.cloned.1.call-done = bf16[4,16,16,4096]{3,2,0,1:T(8,128)(2,1)} async-done(((bf16[4,16,16,1024]{3,2,0,1:T(8,128)(2,1)}), bf16[4,16,16,4096]{3,2,0,1:T(8,128)(2,1)}) %all-gather.3.cloned.1.call-update) | async-done | bytes 8388624 | tf_op jit(solution)/shard_map/all_gather | solution.py:62
  138.5 14.8 %fusion.8 = f32[16,192,4,16]{1,3,2,0:T(8,128)S(1)} fusion(bf16[4,16,16,4096]{3,2,0,1:T(8,128)(2,1)} %all-gather.3.cloned.1.call-done, bf16[16,192,4096]{2,1,0:T(8,128)(2,1)} %param.11), kind=kOutput, calls=%fused_computation.10 | convolution fusion | flops 1610612736 | bytes 34340864 | tf_op jit(solution)/shard_map/slcd,lfd->lfsc/dot_general | solution.py:28
  153.3 15.9 %fusion.17 = bf16[16,192,4,16]{1,3,2,0:T(8,128)(2,1)} fusion(bf16[4,16,16,4096]{3,2,0,1:T(8,128)(2,1)} %all-gather.3.cloned.1.call-done, bf16[16,192,4096]{2,1,0:T(8,128)(2,1)} %param.12, f32[16,192,4,16]{1,3,2,0:T(8,128)S(1)} %fusion.8), kind=kOutput, calls=%fused_computation.13 | convolution fusion | flops 1611792384 | bytes 34734080 | tf_op jit(solution)/shard_map/slcd,lfd->lfsc/dot_general | solution.py:31
  169.2 22.7 %all-gather.5.cloned.1.call-done = bf16[4,16,192,64]{2,3,1,0:T(8,128)(2,1)} async-done(((bf16[1,16,192,64]{2,3,1,0:T(8,128)(2,1)}), bf16[4,16,192,64]{2,3,1,0:T(8,128)(2,1)}) %all-gather.5.cloned.1.call-update) | async-done | bytes 1572880 | tf_op jit(solution)/shard_map/all_gather | solution.py:12
  191.9 3.4 %copy.21 = bf16[16,4,192,64]{2,1,3,0:T(4,128)(2,1)S(1)} copy(bf16[16,4,192,64]{2,3,0,1:T(8,128)(2,1)} %bitcast.76) | data formatting | bytes 3145728 | tf_op jit(solution)/shard_map/reshape | solution.py:11
  195.2 2.9 %reshape_reshape.3 = bf16[16,768,4,16]{1,3,2,0:T(8,128)(2,1)} reshape(bf16[16,4,192,64]{2,1,3,0:T(4,128)(2,1)S(1)} %copy.21) | data formatting | bytes 3145728 | tf_op jit(solution)/shard_map/reshape;reshape | solution.py:35
  198.1 12.8 %convert_bitcast_fusion = bf16[4,16,16,1024]{3,2,0,1:T(8,128)(2,1)S(1)} fusion(bf16[16,768,4,16]{1,3,2,0:T(8,128)(2,1)} %reshape_reshape.3, bf16[16,1024,768]{2,1,0:T(8,128)(2,1)} %param.13), kind=kOutput, calls=%fused_computation.9 | convolution fusion | flops 1611661312 | bytes 28835840 | tf_op jit(solution)/shard_map/lfsc,ldf->slcd/dot_general | solution.py:36
  211.0 1.5 copy.22
  212.5 4.6 %all-to-all-start.1 = ((bf16[4,16,16,1024]{3,2,1,0:T(8,128)(2,1)}), bf16[4,16,16,1024]{3,2,1,0:T(8,128)(2,1)S(1)}, u32[]{:S(2)}, u32[]{:S(2)}) async-start(bf16[4,16,16,1024]{3,2,1,0:T(8,128)(2,1)} %copy.22), calls=%async_computation.1 | async-start | bytes 4194304 | tf_op jit(solution)/shard_map/all_to_all | solution.py:39
  217.1 0.1 copy.26
  217.2 48.5 %all-to-all-done.1 = bf16[4,16,16,1024]{3,2,1,0:T(8,128)(2,1)S(1)} async-done(((bf16[4,16,16,1024]{3,2,1,0:T(8,128)(2,1)}), bf16[4,16,16,1024]{3,2,1,0:T(8,128)(2,1)S(1)}, u32[]{:S(2)}, u32[]{:S(2)}) %all-to-all-start.1) | async-done | bytes 2097184 | tf_op jit(solution)/shard_map/all_to_all | solution.py:39
  265.7 2.0 gather_fusion.1
  267.7 0.4 fusion.20
  268.2 0.7 copy.31
  (14 shorter events, 0.1 us)
Async XLA Ops:
  6.5 132.0 %all-gather.3.cloned.1.call-start = ((), (), s32[]{:S(2)}) async-start(), calls=%async_computation.2 | async-start | bytes 10485760 | tf_op jit(solution)/shard_map/all_gather | solution.py:62
  80.9 110.9 %all-gather.5.cloned.1.call-start = ((), (), s32[]{:S(2)}) async-start(), calls=%async_computation.3 | async-start | bytes 2621440 | tf_op jit(solution)/shard_map/all_gather | solution.py:12
  210.9 6.2 %copy-start = (f32[64,8]{0,1:T(8,128)S(1)}, f32[64,8]{0,1:T(8,128)}, u32[]{:S(2)}) copy-start(f32[64,8]{0,1:T(8,128)} %param.10) | copy-start | bytes 6148
  212.5 53.2 %all-to-all-start.1 = ((bf16[4,16,16,1024]{3,2,1,0:T(8,128)(2,1)}), bf16[4,16,16,1024]{3,2,1,0:T(8,128)(2,1)S(1)}, u32[]{:S(2)}, u32[]{:S(2)}) async-start(bf16[4,16,16,1024]{3,2,1,0:T(8,128)(2,1)} %copy.22), calls=%async_computation.1 | async-start | bytes 4194304 | tf_op jit(solution)/shard_map/all_to_all | solution.py:39
Sparse Core Ops, SparseCore 0:
  81.1 57.3 all-gather.2
  169.3 22.5 all-gather.4
